TPU v7x, 32 devices: a whole 2x2x4 slice. The times are simulated.
32 devices in a mesh: groups: 2 (over y), samp: 4 (over z), feat: 4 (over x, core).
Axes of the slice: x: 2, y: 2, z: 4, core: 2. Of those that a mesh axis runs over, the one named last changes fastest.
Arguments:
- x_blocks: bfloat16 [64, 64, 128, 128], P(('groups', 'samp'), 'feat'), parts along dimension 0, may hold values from -6 to 6
- block_cols: int32 [64, 64], P('groups', 'feat'), parts along dimension 0, may hold values from 0 to 31
- labels: int32 [8192], P('groups'), parts along dimension 0, may hold values from 0 to 63
- group_ids: int32 [8192], P('groups'), parts along dimension 0, may hold values from 0 to 7, as said below
- picks: int32 [3, 32], P(None, 'groups'), parts along dimension 1, may hold values from 0 to 31, as said below
- w_init: float32 [16384, 64], P('feat'), may hold values from -2.253903 to 2.253903
Outputs:
- scores: float32 [8192, 64], P(('groups', 'samp')), parts along dimension 0
- adversary: float32 [16], P('groups'), parts along dimension 0
There are 2 independent parts, one for each index of `groups`. A program takes and returns all parts, laid end to end along the dimension named above; an argument that names none is the same for every part. Nothing has to cross between parts.
Inputs may be any that keep to these rules, and one draw needn't show every extreme that they name: `group_ids`: every row block of 128 samples holds every group at least once. `picks`: the entries of one step are distinct. Row block b is owned by index b // 8 of samp. The k-th aligned block of 4 entries of a step is the list of index k of samp; it names row blocks owned by index k or by the next index along samp (index 0 after the last); between one and 2 entries of each list name the next index's row blocks, exactly 2 in at least one list of every step.
All inputs are finite; a program needn't handle non-finite values.
Results may differ from a plain program's by a relative error of at most 0.00315.
The roundings to bfloat16 on the way count: a program that leaves them out, or rounds other values in their place, can miss the bound.
Values may be sent and summed in bfloat16 or wider, within the bound.
No kernel may reach another device: no remote copies, remote signals or barrier semaphores. Data moves between devices by JAX's collectives and lax.ppermute only.
A program may use at most 64 MiB of HBM per device.

v0:
```python
import jax
import jax.numpy as jnp
from jax import lax
from jax.sharding import PartitionSpec as P

GRP = 8
STEPS = 3
weight_rate = 8.0
adv_rate = 2.0


def per_device(x_blocks, block_cols, labels, group_ids, picks, w_init):
    row_blocks, per_row, block_size, _ = x_blocks.shape
    feat_rows, classes = w_init.shape
    col_blocks = feat_rows // block_size
    total_blocks = block_cols.shape[0]
    feat_count = lax.axis_size("feat")
    my_index = lax.axis_index("samp")
    step_rate = weight_rate * picks.shape[1] / (per_row * feat_count)
    class_range = jnp.arange(classes, dtype=jnp.int32)
    group_range = jnp.arange(GRP, dtype=jnp.int32)
    block_range = jnp.arange(total_blocks, dtype=jnp.int32)
    col_range = jnp.arange(col_blocks, dtype=jnp.int32)
    sample_groups = (group_ids[:, None] == group_range[None, :]).astype(jnp.float32)
    block_groups = jnp.sum(sample_groups.reshape(total_blocks, block_size, GRP), axis=1)
    own_start = my_index * row_blocks
    own_cols = lax.dynamic_slice_in_dim(block_cols, own_start, row_blocks, 0)
    own_labels = lax.dynamic_slice_in_dim(
        labels, own_start * block_size, row_blocks * block_size, 0
    )
    own_groups = lax.dynamic_slice_in_dim(
        group_ids, own_start * block_size, row_blocks * block_size, 0
    )

    def total_logits(x_rows, col_rows, weights_bf):
        tiles = weights_bf.reshape(col_blocks, block_size, classes)[col_rows]
        partial_sum = jnp.einsum(
            "rbij,rbjc->ric", x_rows, tiles, preferred_element_type=jnp.float32
        )
        summed = lax.psum(partial_sum, "feat")
        return summed.reshape(-1, classes)

    def evaluate(row_data, weights_bf, adversary, counts):
        x_rows, col_rows, label_rows, group_rows, mult_rows = row_data
        logits = total_logits(x_rows, col_rows, weights_bf)
        label_hot = (label_rows[:, None] == class_range[None, :]).astype(jnp.float32)
        group_hot = (group_rows[:, None] == group_range[None, :]).astype(jnp.float32)
        log_total = jax.nn.logsumexp(logits, axis=-1)
        cross = log_total - jnp.sum(logits * label_hot, axis=-1)
        probs = jnp.exp(logits - log_total[:, None])
        local_loss = jnp.dot(mult_rows * cross, group_hot, precision=lax.Precision.HIGHEST)
        loss = lax.psum(local_loss, "samp") / counts
        coef = jnp.dot(group_hot, adversary / counts, precision=lax.Precision.HIGHEST) * mult_rows
        dz_rows = (coef[:, None] * (probs - label_hot)).astype(jnp.bfloat16)
        blocks_here = x_rows.shape[0]
        dz_blocks = dz_rows.reshape(blocks_here, block_size, classes)
        grad_tiles = jnp.einsum(
            "rbij,ric->rbjc", x_rows, dz_blocks, preferred_element_type=jnp.float32
        )
        grad_tiles = grad_tiles.reshape(blocks_here * per_row, block_size * classes)
        col_hot = (col_rows.reshape(-1)[:, None] == col_range[None, :]).astype(jnp.float32)
        grad_local = jnp.dot(col_hot.T, grad_tiles, precision=lax.Precision.HIGHEST)
        return (loss, grad_local.reshape(feat_rows, classes))

    def advance(state, grad_local):
        grad_total = lax.psum(grad_local, "samp")
        new_state = state - step_rate * grad_total
        return (new_state, new_state.astype(jnp.bfloat16))

    state = w_init
    weights_bf = w_init.astype(jnp.bfloat16)
    adversary = jnp.full((GRP,), 1.0 / GRP, jnp.float32)
    for step in range(STEPS):
        block_hits = jnp.sum(
            (picks[step][:, None] == block_range[None, :]).astype(jnp.float32), axis=0
        )
        counts = jnp.dot(block_hits, block_groups, precision=lax.Precision.HIGHEST)
        own_hits = lax.dynamic_slice_in_dim(block_hits, own_start, row_blocks, 0)
        row_data = (x_blocks, own_cols, own_labels, own_groups, jnp.repeat(own_hits, block_size))
        loss_first, grad_first = evaluate(row_data, weights_bf, adversary, counts)
        half_state, half_bf = advance(state, grad_first)
        half_adv = jax.nn.softmax(jnp.log(adversary) + adv_rate * loss_first)
        loss_second, grad_second = evaluate(row_data, half_bf, half_adv, counts)
        state, weights_bf = advance(state, grad_second)
        adversary = jax.nn.softmax(jnp.log(adversary) + adv_rate * loss_second)
    return (total_logits(x_blocks, own_cols, weights_bf), adversary)


def solution(mesh):
    in_specs = (
        P(("groups", "samp"), "feat", None, None),
        P("groups", "feat"),
        P("groups"),
        P("groups"),
        P(None, "groups"),
        P("feat", None),
    )
    out_specs = (P(("groups", "samp"), None), P("groups"))
    return jax.shard_map(
        per_device, mesh=mesh, in_specs=in_specs, out_specs=out_specs, check_vma=False
    )
```

profile of v0, /device:TPU:0, one launch (start us, length us, event | category | flops | bytes accessed | tf_op | source)
XLA Modules:
  0.0 842.0 jit_solution(14522523979013200713)
XLA Ops:
  16.2 33.7 %all-reduce.17.cloned.1.call-done = f32[8,128,64]{1,2,0:T(8,128)} async-done(((f32[8,128,64]{1,2,0:T(8,128)}), f32[8,128,64]{1,2,0:T(8,128)}) %all-reduce.17.cloned.1.call-update) | async-done | bytes 262160 | tf_op jit(solution)/shard_map/psum | solution.py:40
  56.8 6.9 copy.85
  63.7 7.9 reshape.440
  80.9 51.9 %all-reduce.19.cloned.1.call-done = f32[4096,64]{0,1:T(8,128)} async-done(((f32[4096,64]{0,1:T(8,128)}), f32[4096,64]{0,1:T(8,128)}) %all-reduce.19.cloned.1.call-update) | async-done | bytes 1048592 | tf_op jit(solution)/shard_map/psum | solution.py:66
  136.4 5.1 convolution_bitcast_fusion.11
  141.5 31.5 %all-reduce.21.cloned.1.call-done = f32[8,128,64]{1,2,0:T(8,128)} async-done(((f32[8,128,64]{1,2,0:T(8,128)}), f32[8,128,64]{1,2,0:T(8,128)}) %all-reduce.21.cloned.1.call-update) | async-done | bytes 262160 | tf_op jit(solution)/shard_map/psum | solution.py:40
  175.8 12.2 %all-reduce.2 = (f32[8]{0:T(128)S(1)}, f32[8]{0:T(128)S(1)}) all-reduce(f32[8]{0:T(128)S(1)} %convolution_bitcast_fusion.21, f32[8]{0:T(128)S(1)} %convolution_bitcast_fusion.20), channel_id=1, replica_groups=mesh['groups'=2,'samp'=4,'feat'=4] {'samp'}, use_global_device_ids=true, to_apply=%region_5.0 | all-reduce | flops 16 | bytes 128 | tf_op jit(solution)/shard_map/psum | solution.py:52
  197.3 6.9 copy.88
  204.2 7.9 reshape.443
  223.3 47.3 %all-reduce.23.cloned.1.call-done = f32[4096,64]{0,1:T(8,128)} async-done(((f32[4096,64]{0,1:T(8,128)}), f32[4096,64]{0,1:T(8,128)}) %all-reduce.23.cloned.1.call-update) | async-done | bytes 1048592 | tf_op jit(solution)/shard_map/psum | solution.py:66
  274.1 5.1 convolution_bitcast_fusion.10
  279.3 31.4 %all-reduce.25.cloned.1.call-done = f32[8,128,64]{1,2,0:T(8,128)} async-done(((f32[8,128,64]{1,2,0:T(8,128)}), f32[8,128,64]{1,2,0:T(8,128)}) %all-reduce.25.cloned.1.call-update) | async-done | bytes 262160 | tf_op jit(solution)/shard_map/psum | solution.py:40
  317.7 6.9 copy.91
  324.6 7.9 reshape.447
  344.0 51.8 %all-reduce.27.cloned.1.call-done = f32[4096,64]{0,1:T(8,128)} async-done(((f32[4096,64]{0,1:T(8,128)}), f32[4096,64]{0,1:T(8,128)}) %all-reduce.27.cloned.1.call-update) | async-done | bytes 1048592 | tf_op jit(solution)/shard_map/psum | solution.py:66
  399.3 5.1 convolution_bitcast_fusion.9
  404.4 31.4 %all-reduce.29.cloned.1.call-done = f32[8,128,64]{1,2,0:T(8,128)} async-done(((f32[8,128,64]{1,2,0:T(8,128)}), f32[8,128,64]{1,2,0:T(8,128)}) %all-reduce.29.cloned.1.call-update) | async-done | bytes 262160 | tf_op jit(solution)/shard_map/psum | solution.py:40
  438.7 11.7 %all-reduce.1 = (f32[8]{0:T(128)S(1)}, f32[8]{0:T(128)S(1)}) all-reduce(f32[8]{0:T(128)S(1)} %convolution_bitcast_fusion.19, f32[8]{0:T(128)S(1)} %convolution_bitcast_fusion.18), channel_id=1, replica_groups=mesh['groups'=2,'samp'=4,'feat'=4] {'samp'}, use_global_device_ids=true, to_apply=%region_23.0 | all-reduce | flops 16 | bytes 128 | tf_op jit(solution)/shard_map/psum | solution.py:52
  455.9 5.0 convolution_bitcast_fusion.2
  460.9 6.9 copy.94
  467.8 7.9 reshape.450
  490.0 46.1 %all-reduce.31.cloned.1.call-done = f32[4096,64]{0,1:T(8,128)} async-done(((f32[4096,64]{0,1:T(8,128)}), f32[4096,64]{0,1:T(8,128)}) %all-reduce.31.cloned.1.call-update) | async-done | bytes 1048592 | tf_op jit(solution)/shard_map/psum | solution.py:66
  544.4 31.2 %all-reduce.33.cloned.1.call-done = f32[8,128,64]{1,2,0:T(8,128)} async-done(((f32[8,128,64]{1,2,0:T(8,128)}), f32[8,128,64]{1,2,0:T(8,128)}) %all-reduce.33.cloned.1.call-update) | async-done | bytes 262160 | tf_op jit(solution)/shard_map/psum | solution.py:40
  582.7 6.9 copy.97
  589.6 7.9 reshape.454
  606.7 51.9 %all-reduce.35.cloned.1.call-done = f32[4096,64]{0,1:T(8,128)} async-done(((f32[4096,64]{0,1:T(8,128)}), f32[4096,64]{0,1:T(8,128)}) %all-reduce.35.cloned.1.call-update) | async-done | bytes 1048592 | tf_op jit(solution)/shard_map/psum | solution.py:66
  665.5 31.5 %all-reduce.37.cloned.1.call-done = f32[8,128,64]{1,2,0:T(8,128)} async-done(((f32[8,128,64]{1,2,0:T(8,128)}), f32[8,128,64]{1,2,0:T(8,128)}) %all-reduce.37.cloned.1.call-update) | async-done | bytes 262160 | tf_op jit(solution)/shard_map/psum | solution.py:40
  699.8 11.7 %all-reduce = (f32[8]{0:T(128)S(1)}, f32[8]{0:T(128)S(1)}) all-reduce(f32[8]{0:T(128)S(1)} %convolution_bitcast_fusion.17, f32[8]{0:T(128)S(1)} %convolution_bitcast_fusion.16), channel_id=1, replica_groups=mesh['groups'=2,'samp'=4,'feat'=4] {'samp'}, use_global_device_ids=true, to_apply=%region_40.0 | all-reduce | flops 16 | bytes 128 | tf_op jit(solution)/shard_map/psum | solution.py:52
  722.0 6.9 copy.100
  728.9 7.9 reshape.457
  747.3 47.9 %all-reduce.39.cloned.1.call-done = f32[4096,64]{0,1:T(8,128)} async-done(((f32[4096,64]{0,1:T(8,128)}), f32[4096,64]{0,1:T(8,128)}) %all-reduce.39.cloned.1.call-update) | async-done | bytes 1048592 | tf_op jit(solution)/shard_map/psum | solution.py:66
  803.8 29.7 %all-reduce.41.cloned.1.call-done = f32[1024,64]{0,1:T(8,128)} async-done(((f32[1024,64]{0,1:T(8,128)}), f32[1024,64]{0,1:T(8,128)}) %all-reduce.41.cloned.1.call-update) | async-done | bytes 262160 | tf_op jit(solution)/shard_map/psum | solution.py:40
  (161 shorter events, 165.7 us)
Async XLA Ops:
  7.2 9.0 %copy-start = (s32[4096]{0:T(1024)S(1)}, s32[4096]{0:T(1024)}, u32[]{:S(2)}) copy-start(s32[4096]{0:T(1024)} %param.8) | copy-start | bytes 49156
  7.2 42.6 %all-reduce.17.cloned.1.call-start = ((), (), s32[]{:S(2)}) async-start(), calls=%async_computation | async-start | bytes 524288 | tf_op jit(solution)/shard_map/psum | solution.py:40
  10.5 4.5 copy-start.7
  10.5 4.7 copy-start.6
  15.0 117.8 %all-reduce.19.cloned.1.call-start = ((), (), s32[]{:S(2)}) async-start(), calls=%async_computation.1 | async-start | bytes 2097152 | tf_op jit(solution)/shard_map/psum | solution.py:66
  75.4 57.4 %copy-start.2 = (f32[4096,64]{0,1:T(8,128)S(1)}, f32[4096,64]{0,1:T(8,128)}, u32[]{:S(2)}) copy-start(f32[4096,64]{0,1:T(8,128)} %param.11) | copy-start | bytes 3145732
  80.8 92.1 %all-reduce.21.cloned.1.call-start = ((), (), s32[]{:S(2)}) async-start(), calls=%async_computation.2 | async-start | bytes 524288 | tf_op jit(solution)/shard_map/psum | solution.py:40
  141.4 129.2 %all-reduce.23.cloned.1.call-start = ((), (), s32[]{:S(2)}) async-start(), calls=%async_computation.3 | async-start | bytes 2097152 | tf_op jit(solution)/shard_map/psum | solution.py:66
  221.3 89.4 %all-reduce.25.cloned.1.call-start = ((), (), s32[]{:S(2)}) async-start(), calls=%async_computation.4 | async-start | bytes 524288 | tf_op jit(solution)/shard_map/psum | solution.py:40
  279.2 116.5 %all-reduce.27.cloned.1.call-start = ((), (), s32[]{:S(2)}) async-start(), calls=%async_computation.5 | async-start | bytes 2097152 | tf_op jit(solution)/shard_map/psum | solution.py:66
  337.3 58.4 %copy-start.3 = (f32[4096,64]{0,1:T(8,128)S(1)}, f32[4096,64]{0,1:T(8,128)}, u32[]{:S(2)}) copy-start(f32[4096,64]{0,1:T(8,128)} %all-reduce.23.cloned.1.call-done) | copy-start | bytes 3145732
  343.7 92.1 %all-reduce.29.cloned.1.call-start = ((), (), s32[]{:S(2)}) async-start(), calls=%async_computation.6 | async-start | bytes 524288 | tf_op jit(solution)/shard_map/psum | solution.py:40
  404.4 131.7 %all-reduce.31.cloned.1.call-start = ((), (), s32[]{:S(2)}) async-start(), calls=%async_computation.7 | async-start | bytes 2097152 | tf_op jit(solution)/shard_map/psum | solution.py:66
  486.8 88.9 %all-reduce.33.cloned.1.call-start = ((), (), s32[]{:S(2)}) async-start(), calls=%async_computation.8 | async-start | bytes 524288 | tf_op jit(solution)/shard_map/psum | solution.py:40
  544.1 114.6 %all-reduce.35.cloned.1.call-start = ((), (), s32[]{:S(2)}) async-start(), calls=%async_computation.9 | async-start | bytes 2097152 | tf_op jit(solution)/shard_map/psum | solution.py:66
  601.3 57.4 %copy-start.4 = (f32[4096,64]{0,1:T(8,128)S(1)}, f32[4096,64]{0,1:T(8,128)}, u32[]{:S(2)}) copy-start(f32[4096,64]{0,1:T(8,128)} %get-tuple-element.29) | copy-start | bytes 3145732
  606.7 90.3 %all-reduce.37.cloned.1.call-start = ((), (), s32[]{:S(2)}) async-start(), calls=%async_computation.10 | async-start | bytes 524288 | tf_op jit(solution)/shard_map/psum | solution.py:40
  665.4 129.8 %all-reduce.39.cloned.1.call-start = ((), (), s32[]{:S(2)}) async-start(), calls=%async_computation.11 | async-start | bytes 2097152 | tf_op jit(solution)/shard_map/psum | solution.py:66
  740.6 54.6 %copy-start.5 = (f32[4096,64]{0,1:T(8,128)S(1)}, f32[4096,64]{0,1:T(8,128)}, u32[]{:S(2)}) copy-start(f32[4096,64]{0,1:T(8,128)} %get-tuple-element.29) | copy-start | bytes 3145732
  746.0 87.6 %all-reduce.41.cloned.1.call-start = ((), (), s32[]{:S(2)}) async-start(), calls=%async_computation.12 | async-start | bytes 524288 | tf_op jit(solution)/shard_map/psum | solution.py:40
  796.6 38.6 %copy-start.1 = (s32[4096]{0:T(1024)S(1)}, s32[4096]{0:T(1024)}, u32[]{:S(2)}) copy-start(s32[4096]{0:T(1024)} %param.8) | copy-start | bytes 49156
Sparse Core Ops, SparseCore 0:
  15.1 34.6 all-reduce.16
  80.9 51.8 all-reduce.18
  141.6 31.3 all-reduce.20
  221.4 49.1 all-reduce.22
  279.3 31.3 all-reduce.24
  343.9 51.8 all-reduce.26
  404.5 31.3 all-reduce.28
  486.9 49.1 all-reduce.30
  544.2 31.4 all-reduce.32
  606.8 51.8 all-reduce.34
  665.5 31.3 all-reduce.36
  746.1 49.0 all-reduce.38
  802.2 31.3 all-reduce.40
where the time goes:
time: 851 us; the launch traced here: 842 us
  waiting for transfers between devices  518 us (61%)
  local copies, waits for them, and re-layouts  136 us (16%)
  matrix products  98.5 us (12%)
  other arithmetic  38.8 us (5%)
  blocking collectives  35.5 us (4%)
  between operations  14.6 us (2%)
    psum x6, waiting for transfers between devices, advance(): grad_total = lax.psum(grad_local, 'samp')  297 us
    psum x7, waiting for transfers between devices, total_logits(): summed = lax.psum(partial_sum, 'feat')  220 us
    reshape x6, local copies, waits for them, and re-layouts, evaluate(): grad_tiles = grad_tiles.reshape(blocks_here * per_row, block_size * classes)  47.3 us
    dot_general x6, local copies, waits for them, and re-layouts, evaluate(): jnp.einsum('rbij,ric->rbjc', x_rows, dz_blocks, preferred_element_type=jn...  41.4 us
    psum x3, blocking collectives, evaluate(): loss = lax.psum(local_loss, 'samp') / counts  35.5 us
    reshape x12, local copies, waits for them, and re-layouts, evaluate(): return (loss, grad_local.reshape(feat_rows, classes))  34.1 us
    dot_general x7, matrix products, total_logits(): jnp.einsum('rbij,rbjc->ric', x_rows, tiles, preferred_element_type=jnp.fl...  32.2 us
    dot_general x6, matrix products, evaluate(): jnp.einsum('rbij,ric->rbjc', x_rows, dz_blocks, preferred_element_type=jn...  29.8 us
  transfers between devices with their start and end apart: 13, of which 13 were waited for; matrix products, arithmetic and copies ran while one was open for 1% of the time, Pallas kernels for 0%

commit v1 on v0

--- a/solution.py
+++ b/solution.py
@@ -7,6 +7,15 @@
 STEPS = 3
 weight_rate = 8.0
 adv_rate = 2.0
+
+
+def add_in_pairs(x, axis):
+    size = lax.axis_size(axis)
+    total, reach = (x, 1)
+    while reach < size:
+        total = total + lax.ppermute(total, axis, [(i, i ^ reach) for i in range(size)])
+        reach = 2 * reach
+    return total
 
 
 def per_device(x_blocks, block_cols, labels, group_ids, picks, w_init):
@@ -37,7 +46,7 @@
         partial_sum = jnp.einsum(
             "rbij,rbjc->ric", x_rows, tiles, preferred_element_type=jnp.float32
         )
-        summed = lax.psum(partial_sum, "feat")
+        summed = add_in_pairs(partial_sum, "feat")
         return summed.reshape(-1, classes)
 
     def evaluate(row_data, weights_bf, adversary, counts):

time: 851 us -> 676 us (0.79)
  waiting for transfers between devices: 518 us -> 355 us
  starting transfers between devices: 0.92 us -> 14 us
  other arithmetic: 38.8 us -> 28.6 us
  matrix products: 98.5 us -> 89.8 us
    psum x7 -> x0, waiting for transfers between devices: 220 us -> none  [total_logits(): summed = lax.psum(partial_sum, 'feat')]
    ppermute x0 -> x14, waiting for transfers between devices: none -> 49 us  [add_in_pairs(): lax.ppermute(total, axis, [(i, i ^ reach) for i in range(size)])]
    ppermute x0 -> x14, starting transfers between devices: none -> 13.3 us  [add_in_pairs(): lax.ppermute(total, axis, [(i, i ^ reach) for i in range(size)])]
    psum x6, waiting for transfers between devices: 297 us -> 306 us  [advance(): grad_total = lax.psum(grad_local, 'samp')]
  transfers between devices with their start and end apart: 13 -> 20, of which waited for: 13 -> 19; matrix products, arithmetic and copies ran while one was open for 1% -> 1% of each run, Pallas kernels for 0% -> 0%
where the time goes in v1:
time: 676 us; the launch traced here: 667 us
  waiting for transfers between devices  355 us (53%)
  local copies, waits for them, and re-layouts  134 us (20%)
  matrix products  89.8 us (13%)
  blocking collectives  31 us (5%)
  other arithmetic  28.6 us (4%)
  between operations  15.1 us (2%)
  starting transfers between devices  14 us (2%)
    psum x6, waiting for transfers between devices, advance(): grad_total = lax.psum(grad_local, 'samp')  306 us
    ppermute x14, waiting for transfers between devices, add_in_pairs(): lax.ppermute(total, axis, [(i, i ^ reach) for i in range(size)])  49 us
    reshape x6, local copies, waits for them, and re-layouts, evaluate(): grad_tiles = grad_tiles.reshape(blocks_here * per_row, block_size * classes)  47.3 us
    dot_general x6, local copies, waits for them, and re-layouts, evaluate(): jnp.einsum('rbij,ric->rbjc', x_rows, dz_blocks, preferred_element_type=jn...  41.4 us
    reshape x12, local copies, waits for them, and re-layouts, evaluate(): return (loss, grad_local.reshape(feat_rows, classes))  34.1 us
    psum x3, blocking collectives, evaluate(): loss = lax.psum(local_loss, 'samp') / counts  31 us
    dot_general x7, matrix products, total_logits(): jnp.einsum('rbij,rbjc->ric', x_rows, tiles, preferred_element_type=jnp.fl...  28.2 us
    dot_general x6, matrix products, evaluate(): jnp.einsum('rbij,ric->rbjc', x_rows, dz_blocks, preferred_element_type=jn...  24.9 us
  transfers between devices with their start and end apart: 20, of which 19 were waited for; matrix products, arithmetic and copies ran while one was open for 1% of the time, Pallas kernels for 0%

profile of v1, /device:TPU:0, one launch (start us, length us, event | category | flops | bytes accessed | tf_op | source)
XLA Modules:
  0.0 667.2 jit_solution(16535051827249323139)
XLA Ops:
  19.2 6.3 collective-permute-done.1
  25.6 4.9 convolution_bitcast_fusion.5
  30.5 6.9 %copy.85 = f32[8,16,128,64]{3,2,1,0:T(8,128)} copy(f32[8,16,128,64]{2,3,1,0:T(8,128)} %convolution_bitcast_fusion.5) | data formatting | bytes 8388608 | tf_op jit(solution)/shard_map/rbij,ric->rbjc/dot_general | solution.py:66
  37.4 7.9 %reshape.440 = f32[128,8192]{1,0:T(8,128)} reshape(f32[8,16,128,64]{3,2,1,0:T(8,128)} %copy.85) | data formatting | bytes 8388608 | tf_op jit(solution)/shard_map/reshape | solution.py:69
  54.6 53.4 %all-reduce.10.cloned.1.call-done = f32[4096,64]{0,1:T(8,128)} async-done(((f32[4096,64]{0,1:T(8,128)}), f32[4096,64]{0,1:T(8,128)}) %all-reduce.10.cloned.1.call-update) | async-done | bytes 1048592 | tf_op jit(solution)/shard_map/psum | solution.py:75
  119.1 6.9 %collective-permute-done.3 = f32[8,128,64]{1,2,0:T(8,128)S(1)} collective-permute-done((f32[8,128,64]{1,2,0:T(8,128)S(1)}, f32[8,128,64]{1,2,0:T(8,128)S(1)}, u32[]{:S(2)}, u32[]{:S(2)}) %collective-permute-start.3) | collective-permute-done | bytes 262176 | tf_op jit(solution)/shard_map/ppermute | solution.py:16
  127.0 10.3 %all-reduce.2 = (f32[8]{0:T(128)S(1)}, f32[8]{0:T(128)S(1)}) all-reduce(f32[8]{0:T(128)S(1)} %convolution_bitcast_fusion.21, f32[8]{0:T(128)S(1)} %convolution_bitcast_fusion.20), channel_id=1, replica_groups=mesh['groups'=2,'samp'=4,'feat'=4] {'samp'}, use_global_device_ids=true, to_apply=%region_4.0 | all-reduce | flops 16 | bytes 128 | tf_op jit(solution)/shard_map/psum | solution.py:61
  141.7 4.9 convolution_bitcast_fusion.4
  146.6 6.9 %copy.88 = f32[8,16,128,64]{3,2,1,0:T(8,128)} copy(f32[8,16,128,64]{2,3,1,0:T(8,128)} %convolution_bitcast_fusion.4) | data formatting | bytes 8388608 | tf_op jit(solution)/shard_map/rbij,ric->rbjc/dot_general | solution.py:66
  153.5 7.9 %reshape.443 = f32[128,8192]{1,0:T(8,128)} reshape(f32[8,16,128,64]{3,2,1,0:T(8,128)} %copy.88) | data formatting | bytes 8388608 | tf_op jit(solution)/shard_map/reshape | solution.py:69
  170.7 50.0 %all-reduce.12.cloned.1.call-done = f32[4096,64]{0,1:T(8,128)} async-done(((f32[4096,64]{0,1:T(8,128)}), f32[4096,64]{0,1:T(8,128)}) %all-reduce.12.cloned.1.call-update) | async-done | bytes 1048592 | tf_op jit(solution)/shard_map/psum | solution.py:75
  233.6 5.1 collective-permute-done.5
  241.6 6.9 %copy.91 = f32[8,16,128,64]{3,2,1,0:T(8,128)} copy(f32[8,16,128,64]{2,3,1,0:T(8,128)} %convolution_bitcast_fusion.3) | data formatting | bytes 8388608 | tf_op jit(solution)/shard_map/rbij,ric->rbjc/dot_general | solution.py:66
  248.5 7.9 %reshape.447 = f32[128,8192]{1,0:T(8,128)} reshape(f32[8,16,128,64]{3,2,1,0:T(8,128)} %copy.91) | data formatting | bytes 8388608 | tf_op jit(solution)/shard_map/reshape | solution.py:69
  256.4 4.8 fusion.67
  267.9 51.1 %all-reduce.14.cloned.1.call-done = f32[4096,64]{0,1:T(8,128)} async-done(((f32[4096,64]{0,1:T(8,128)}), f32[4096,64]{0,1:T(8,128)}) %all-reduce.14.cloned.1.call-update) | async-done | bytes 1048592 | tf_op jit(solution)/shard_map/psum | solution.py:75
  330.1 6.9 %collective-permute-done.7 = f32[8,128,64]{1,2,0:T(8,128)S(1)} collective-permute-done((f32[8,128,64]{1,2,0:T(8,128)S(1)}, f32[8,128,64]{1,2,0:T(8,128)S(1)}, u32[]{:S(2)}, u32[]{:S(2)}) %collective-permute-start.7) | collective-permute-done | bytes 262176 | tf_op jit(solution)/shard_map/ppermute | solution.py:16
  338.0 10.2 %all-reduce.1 = (f32[8]{0:T(128)S(1)}, f32[8]{0:T(128)S(1)}) all-reduce(f32[8]{0:T(128)S(1)} %convolution_bitcast_fusion.19, f32[8]{0:T(128)S(1)} %convolution_bitcast_fusion.18), channel_id=1, replica_groups=mesh['groups'=2,'samp'=4,'feat'=4] {'samp'}, use_global_device_ids=true, to_apply=%region_20.0 | all-reduce | flops 16 | bytes 128 | tf_op jit(solution)/shard_map/psum | solution.py:61
  353.8 4.9 convolution_bitcast_fusion.2
  358.7 6.9 %copy.94 = f32[8,16,128,64]{3,2,1,0:T(8,128)} copy(f32[8,16,128,64]{2,3,1,0:T(8,128)} %convolution_bitcast_fusion.2) | data formatting | bytes 8388608 | tf_op jit(solution)/shard_map/rbij,ric->rbjc/dot_general | solution.py:66
  365.6 7.9 %reshape.450 = f32[128,8192]{1,0:T(8,128)} reshape(f32[8,16,128,64]{3,2,1,0:T(8,128)} %copy.94) | data formatting | bytes 8388608 | tf_op jit(solution)/shard_map/reshape | solution.py:69
  384.9 49.8 %all-reduce.16.cloned.1.call-done = f32[4096,64]{0,1:T(8,128)} async-done(((f32[4096,64]{0,1:T(8,128)}), f32[4096,64]{0,1:T(8,128)}) %all-reduce.16.cloned.1.call-update) | async-done | bytes 1048592 | tf_op jit(solution)/shard_map/psum | solution.py:75
  447.2 5.4 collective-permute-done.9
  455.4 6.9 %copy.97 = f32[8,16,128,64]{3,2,1,0:T(8,128)} copy(f32[8,16,128,64]{2,3,1,0:T(8,128)} %convolution_bitcast_fusion.1) | data formatting | bytes 8388608 | tf_op jit(solution)/shard_map/rbij,ric->rbjc/dot_general | solution.py:66
  462.3 7.9 %reshape.454 = f32[128,8192]{1,0:T(8,128)} reshape(f32[8,16,128,64]{3,2,1,0:T(8,128)} %copy.97) | data formatting | bytes 8388608 | tf_op jit(solution)/shard_map/reshape | solution.py:69
  479.5 51.3 %all-reduce.18.cloned.1.call-done = f32[4096,64]{0,1:T(8,128)} async-done(((f32[4096,64]{0,1:T(8,128)}), f32[4096,64]{0,1:T(8,128)}) %all-reduce.18.cloned.1.call-update) | async-done | bytes 1048592 | tf_op jit(solution)/shard_map/psum | solution.py:75
  540.0 6.9 %collective-permute-done.11 = f32[8,128,64]{1,2,0:T(8,128)S(1)} collective-permute-done((f32[8,128,64]{1,2,0:T(8,128)S(1)}, f32[8,128,64]{1,2,0:T(8,128)S(1)}, u32[]{:S(2)}, u32[]{:S(2)}) %collective-permute-start.11) | collective-permute-done | bytes 262176 | tf_op jit(solution)/shard_map/ppermute | solution.py:16
  547.9 10.5 %all-reduce = (f32[8]{0:T(128)S(1)}, f32[8]{0:T(128)S(1)}) all-reduce(f32[8]{0:T(128)S(1)} %convolution_bitcast_fusion.17, f32[8]{0:T(128)S(1)} %convolution_bitcast_fusion.16), channel_id=1, replica_groups=mesh['groups'=2,'samp'=4,'feat'=4] {'samp'}, use_global_device_ids=true, to_apply=%region_35.0 | all-reduce | flops 16 | bytes 128 | tf_op jit(solution)/shard_map/psum | solution.py:61
  564.0 4.9 convolution_bitcast_fusion
  568.8 6.9 %copy.100 = f32[8,16,128,64]{3,2,1,0:T(8,128)} copy(f32[8,16,128,64]{2,3,1,0:T(8,128)} %convolution_bitcast_fusion) | data formatting | bytes 8388608 | tf_op jit(solution)/shard_map/rbij,ric->rbjc/dot_general | solution.py:66
  575.8 7.9 %reshape.457 = f32[128,8192]{1,0:T(8,128)} reshape(f32[8,16,128,64]{3,2,1,0:T(8,128)} %copy.100) | data formatting | bytes 8388608 | tf_op jit(solution)/shard_map/reshape | solution.py:69
  592.8 50.1 %all-reduce.20.cloned.1.call-done = f32[4096,64]{0,1:T(8,128)} async-done(((f32[4096,64]{0,1:T(8,128)}), f32[4096,64]{0,1:T(8,128)}) %all-reduce.20.cloned.1.call-update) | async-done | bytes 1048592 | tf_op jit(solution)/shard_map/psum | solution.py:75
  (178 shorter events, 164.7 us)
Async XLA Ops:
  7.2 11.7 %copy-start = (s32[4096]{0:T(1024)S(1)}, s32[4096]{0:T(1024)}, u32[]{:S(2)}) copy-start(s32[4096]{0:T(1024)} %param.8) | copy-start | bytes 49156
  7.2 100.8 %all-reduce.10.cloned.1.call-start = ((), (), s32[]{:S(2)}) async-start(), calls=%async_computation | async-start | bytes 2097152 | tf_op jit(solution)/shard_map/psum | solution.py:75
  10.5 4.3 copy-start.9
  10.5 4.4 copy-start.8
  14.2 1.7 collective-permute-start
  16.0 9.5 %collective-permute-start.1 = (f32[8,128,64]{1,2,0:T(8,128)S(1)}, f32[8,128,64]{1,2,0:T(8,128)S(1)}, u32[]{:S(2)}, u32[]{:S(2)}) collective-permute-start(f32[8,128,64]{1,2,0:T(8,128)S(1)} %add.154), channel_id=1, source_target_pairs={{0,2},{1,3},{2,0},{3,1},{4,6},{5,7},{6,4},{7,5},{8,10},{9,11},{10,... | collective-permute-start | bytes 786440 | tf_op jit(solution)/shard_map/ppermute | solution.py:16
  49.1 58.9 %copy-start.4 = (f32[4096,64]{0,1:T(8,128)S(1)}, f32[4096,64]{0,1:T(8,128)}, u32[]{:S(2)}) copy-start(f32[4096,64]{0,1:T(8,128)} %param.11) | copy-start | bytes 3145732
  54.5 166.2 %all-reduce.12.cloned.1.call-start = ((), (), s32[]{:S(2)}) async-start(), calls=%async_computation.1 | async-start | bytes 2097152 | tf_op jit(solution)/shard_map/psum | solution.py:75
  115.9 1.6 collective-permute-start.2
  117.5 8.4 %collective-permute-start.3 = (f32[8,128,64]{1,2,0:T(8,128)S(1)}, f32[8,128,64]{1,2,0:T(8,128)S(1)}, u32[]{:S(2)}, u32[]{:S(2)}) collective-permute-start(f32[8,128,64]{1,2,0:T(8,128)S(1)} %add.158), channel_id=1, source_target_pairs={{0,2},{1,3},{2,0},{3,1},{4,6},{5,7},{6,4},{7,5},{8,10},{9,11},{10,... | collective-permute-start | bytes 786440 | tf_op jit(solution)/shard_map/ppermute | solution.py:16
  170.6 148.4 %all-reduce.14.cloned.1.call-start = ((), (), s32[]{:S(2)}) async-start(), calls=%async_computation.2 | async-start | bytes 2097152 | tf_op jit(solution)/shard_map/psum | solution.py:75
  224.2 14.7 %copy-start.2 = (bf16[8,16,128,128]{3,2,1,0:T(8,128)(2,1)S(1)}, bf16[8,16,128,128]{3,2,1,0:T(8,128)(2,1)}, u32[]{:S(2)}) copy-start(bf16[8,16,128,128]{3,2,1,0:T(8,128)(2,1)} %param.6) | copy-start | bytes 12582916
  228.7 1.6 collective-permute-start.4
  230.4 8.4 %collective-permute-start.5 = (f32[8,128,64]{1,2,0:T(8,128)S(1)}, f32[8,128,64]{1,2,0:T(8,128)S(1)}, u32[]{:S(2)}, u32[]{:S(2)}) collective-permute-start(f32[8,128,64]{1,2,0:T(8,128)S(1)} %add.162), channel_id=1, source_target_pairs={{0,2},{1,3},{2,0},{3,1},{4,6},{5,7},{6,4},{7,5},{8,10},{9,11},{10,... | collective-permute-start | bytes 786440 | tf_op jit(solution)/shard_map/ppermute | solution.py:16
  261.2 57.8 %copy-start.5 = (f32[4096,64]{0,1:T(8,128)S(1)}, f32[4096,64]{0,1:T(8,128)}, u32[]{:S(2)}) copy-start(f32[4096,64]{0,1:T(8,128)} %all-reduce.12.cloned.1.call-done) | copy-start | bytes 3145732
  267.6 167.0 %all-reduce.16.cloned.1.call-start = ((), (), s32[]{:S(2)}) async-start(), calls=%async_computation.3 | async-start | bytes 2097152 | tf_op jit(solution)/shard_map/psum | solution.py:75
  326.9 1.6 collective-permute-start.6
  328.6 8.4 %collective-permute-start.7 = (f32[8,128,64]{1,2,0:T(8,128)S(1)}, f32[8,128,64]{1,2,0:T(8,128)S(1)}, u32[]{:S(2)}, u32[]{:S(2)}) collective-permute-start(f32[8,128,64]{1,2,0:T(8,128)S(1)} %add.167), channel_id=1, source_target_pairs={{0,2},{1,3},{2,0},{3,1},{4,6},{5,7},{6,4},{7,5},{8,10},{9,11},{10,... | collective-permute-start | bytes 786440 | tf_op jit(solution)/shard_map/ppermute | solution.py:16
  384.6 146.2 %all-reduce.18.cloned.1.call-start = ((), (), s32[]{:S(2)}) async-start(), calls=%async_computation.4 | async-start | bytes 2097152 | tf_op jit(solution)/shard_map/psum | solution.py:75
  438.3 14.5 %copy-start.3 = (bf16[8,16,128,128]{3,2,1,0:T(8,128)(2,1)S(1)}, bf16[8,16,128,128]{3,2,1,0:T(8,128)(2,1)}, u32[]{:S(2)}) copy-start(bf16[8,16,128,128]{3,2,1,0:T(8,128)(2,1)} %param.6) | copy-start | bytes 12582916
  442.1 1.7 collective-permute-start.8
  443.8 8.7 %collective-permute-start.9 = (f32[8,128,64]{1,2,0:T(8,128)S(1)}, f32[8,128,64]{1,2,0:T(8,128)S(1)}, u32[]{:S(2)}, u32[]{:S(2)}) collective-permute-start(f32[8,128,64]{1,2,0:T(8,128)S(1)} %add.172), channel_id=1, source_target_pairs={{0,2},{1,3},{2,0},{3,1},{4,6},{5,7},{6,4},{7,5},{8,10},{9,11},{10,... | collective-permute-start | bytes 786440 | tf_op jit(solution)/shard_map/ppermute | solution.py:16
  474.0 56.8 %copy-start.6 = (f32[4096,64]{0,1:T(8,128)S(1)}, f32[4096,64]{0,1:T(8,128)}, u32[]{:S(2)}) copy-start(f32[4096,64]{0,1:T(8,128)} %get-tuple-element.33) | copy-start | bytes 3145732
  479.4 163.5 %all-reduce.20.cloned.1.call-start = ((), (), s32[]{:S(2)}) async-start(), calls=%async_computation.5 | async-start | bytes 2097152 | tf_op jit(solution)/shard_map/psum | solution.py:75
  536.9 1.6 collective-permute-start.10
  538.5 8.4 %collective-permute-start.11 = (f32[8,128,64]{1,2,0:T(8,128)S(1)}, f32[8,128,64]{1,2,0:T(8,128)S(1)}, u32[]{:S(2)}, u32[]{:S(2)}) collective-permute-start(f32[8,128,64]{1,2,0:T(8,128)S(1)} %add.177), channel_id=1, source_target_pairs={{0,2},{1,3},{2,0},{3,1},{4,6},{5,7},{6,4},{7,5},{8,10},{9,11},{10,... | collective-permute-start | bytes 786440 | tf_op jit(solution)/shard_map/ppermute | solution.py:16
  587.5 55.5 %copy-start.7 = (f32[4096,64]{0,1:T(8,128)S(1)}, f32[4096,64]{0,1:T(8,128)}, u32[]{:S(2)}) copy-start(f32[4096,64]{0,1:T(8,128)} %get-tuple-element.33) | copy-start | bytes 3145732
  644.3 15.5 %copy-start.1 = (s32[4096]{0:T(1024)S(1)}, s32[4096]{0:T(1024)}, u32[]{:S(2)}) copy-start(s32[4096]{0:T(1024)} %param.8) | copy-start | bytes 49156
  649.0 1.6 collective-permute-start.12
  650.7 8.4 %collective-permute-start.13 = (f32[8,128,64]{1,2,0:T(8,128)S(1)}, f32[8,128,64]{1,2,0:T(8,128)S(1)}, u32[]{:S(2)}, u32[]{:S(2)}) collective-permute-start(f32[8,128,64]{1,2,0:T(8,128)S(1)} %add.180), channel_id=1, source_target_pairs={{0,2},{1,3},{2,0},{3,1},{4,6},{5,7},{6,4},{7,5},{8,10},{9,11},{10,... | collective-permute-start | bytes 786440 | tf_op jit(solution)/shard_map/ppermute | solution.py:16
Sparse Core Ops, SparseCore 0:
  54.6 53.3 all-reduce.9
  170.7 49.9 all-reduce.11
  267.8 51.1 all-reduce.13
  384.7 49.9 all-reduce.15
  479.6 51.1 all-reduce.17
  593.0 49.9 all-reduce.19
